TPU v7x, 256 devices: a whole 4x4x8 slice. The times are simulated.
256 devices in a mesh: seq: 32 (over z, x_lo, core), chan: 8 (over x_hi, y).
Axes of the slice: x: 4 (x_hi: 2, x_lo: 2; x = x_hi * 2 + x_lo), y: 4, z: 8, core: 2. Of those that a mesh axis runs over, the one named last changes fastest.
Arguments:
- q_gate: float32 [16384, 2048], P('seq', 'chan'), may hold values from -6 to 6
- k_gate: float32 [16384, 2048], P('seq', 'chan'), may hold values from -6 to 6
- values: float32 [16384, 2048], P('seq', 'chan'), may hold values from -6 to 6
- filter_raw: float32 [16384, 128], P('seq'), may hold values from -6 to 6
- grad_out: float32 [16384, 2048], P('seq', 'chan'), may hold values from -6 to 6
Outputs:
- grad_q: float32 [16384, 2048], P('seq', 'chan')
- grad_k: float32 [16384, 2048], P('seq', 'chan')
- grad_v: float32 [16384, 2048], P('seq', 'chan')
- grad_filter: float32 [16384, 128], P('seq')
All inputs are finite; a program needn't handle non-finite values.
Results may differ from a plain program's by a relative error of at most 0.0001.
Values sent between devices are 32-bit elements; how exact they have to be, the bound alone decides.
No kernel may reach another device: no remote copies, remote signals or barrier semaphores. Data moves between devices by JAX's collectives and lax.ppermute only.
A program may use at most 64 MiB of HBM per device.

v0:
```python
import math
import jax
import jax.numpy as jnp
from jax import lax
from jax.sharding import PartitionSpec as P


def product_hi(form, left, right):
    return jnp.einsum(form, left, right, precision=lax.Precision.HIGHEST)


def angle_table(first, second, modulus):
    counts = first[:, None] * second[None, :] % modulus
    angles = counts.astype(jnp.float32) * (2.0 * math.pi / modulus)
    return (jnp.cos(angles), jnp.sin(angles))


def forward_transform(block, shards, offset_base, cos_coarse, sin_coarse, cos_fine, sin_fine):
    seq_len = block.shape[0]
    coarse = 2 * shards
    total = coarse * seq_len
    share = seq_len // shards
    spread = lax.all_to_all(block[None], "seq", split_axis=1, concat_axis=0, tiled=True)
    real_part = product_hi("kn,nbw->kbw", cos_coarse, spread)
    imag_part = -product_hi("kn,nbw->kbw", sin_coarse, spread)
    offsets = offset_base * share + jnp.arange(share, dtype=jnp.int32)
    freq_rows = jnp.arange(coarse, dtype=jnp.int32)
    twist_cos, twist_sin = angle_table(freq_rows, offsets, total)
    twist_cos = twist_cos[:, :, None]
    twist_sin = twist_sin[:, :, None]
    turned_real = real_part * twist_cos + imag_part * twist_sin
    turned_imag = imag_part * twist_cos - real_part * twist_sin
    moved_real, moved_imag = (
        lax.all_to_all(turned_real, "seq", split_axis=0, concat_axis=1, tiled=True),
        lax.all_to_all(turned_imag, "seq", split_axis=0, concat_axis=1, tiled=True),
    )
    spec_real = product_hi("kn,tnw->tkw", cos_fine, moved_real) + product_hi(
        "kn,tnw->tkw", sin_fine, moved_imag
    )
    spec_imag = product_hi("kn,tnw->tkw", cos_fine, moved_imag) - product_hi(
        "kn,tnw->tkw", sin_fine, moved_real
    )
    return (spec_real, spec_imag)


def inverse_transform(spec_real, spec_imag, shards, offset_base, cos_fine, sin_fine):
    seq_len = spec_real.shape[1]
    coarse = 2 * shards
    total = coarse * seq_len
    part_real = product_hi("nk,tkw->tnw", cos_fine, spec_real) - product_hi(
        "nk,tkw->tnw", sin_fine, spec_imag
    )
    part_imag = product_hi("nk,tkw->tnw", cos_fine, spec_imag) + product_hi(
        "nk,tkw->tnw", sin_fine, spec_real
    )
    local_freq = 2 * offset_base + jnp.arange(2, dtype=jnp.int32)
    positions = jnp.arange(seq_len, dtype=jnp.int32)
    twist_cos, twist_sin = angle_table(local_freq, positions, total)
    twist_cos = twist_cos[:, :, None]
    twist_sin = twist_sin[:, :, None]
    turned_real = part_real * twist_cos - part_imag * twist_sin
    turned_imag = part_imag * twist_cos + part_real * twist_sin
    moved_real, moved_imag = (
        lax.all_to_all(turned_real, "seq", split_axis=1, concat_axis=0, tiled=True),
        lax.all_to_all(turned_imag, "seq", split_axis=1, concat_axis=0, tiled=True),
    )
    rows_out = jnp.arange(shards, dtype=jnp.int32)
    freq_rows = jnp.arange(coarse, dtype=jnp.int32)
    back_cos, back_sin = angle_table(rows_out, freq_rows, coarse)
    spatial = (
        product_hi("nk,kbw->nbw", back_cos, moved_real)
        - product_hi("nk,kbw->nbw", back_sin, moved_imag)
    ) * (1.0 / total)
    placed = lax.all_to_all(spatial, "seq", split_axis=0, concat_axis=1, tiled=True)
    return placed[0]


def local(q_gate, k_gate, values, filter_raw, grad_out):
    seq_len = q_gate.shape[0]
    width = q_gate.shape[1]
    nfilt = filter_raw.shape[1]
    shards = lax.axis_size("seq")
    offset_base = lax.axis_index("seq")
    scale = float(seq_len * shards) ** (-0.5)
    coarse_rows = jnp.arange(2 * shards, dtype=jnp.int32)
    cos_coarse, sin_coarse = angle_table(
        coarse_rows, jnp.arange(shards, dtype=jnp.int32), 2 * shards
    )
    fine_rows = jnp.arange(seq_len, dtype=jnp.int32)
    cos_fine, sin_fine = angle_table(fine_rows, fine_rows, seq_len)
    gated = k_gate * values
    grad_conv = grad_out * q_gate
    filt = filter_raw * scale

    def forward(block):
        return forward_transform(
            block, shards, offset_base, cos_coarse, sin_coarse, cos_fine, sin_fine
        )

    def inverse(real_part, imag_part):
        return inverse_transform(real_part, imag_part, shards, offset_base, cos_fine, sin_fine)

    gated_real, gated_imag = forward(gated)
    grad_real, grad_imag = forward(grad_conv)
    filt_real, filt_imag = forward(filt)
    repeats = width // nfilt
    wide_real = jnp.tile(filt_real, (1, 1, repeats))
    wide_imag = jnp.tile(filt_imag, (1, 1, repeats))
    conv_real = wide_real * gated_real - wide_imag * gated_imag
    conv_imag = wide_real * gated_imag + wide_imag * gated_real
    back_real = wide_real * grad_real + wide_imag * grad_imag
    back_imag = wide_real * grad_imag - wide_imag * grad_real
    corr_real = gated_real * grad_real + gated_imag * grad_imag
    corr_imag = gated_real * grad_imag - gated_imag * grad_real
    folded_real = jnp.sum(corr_real.reshape(2, seq_len, repeats, nfilt), axis=2)
    folded_imag = jnp.sum(corr_imag.reshape(2, seq_len, repeats, nfilt), axis=2)
    filter_real, filter_imag = (folded_real, folded_imag)
    conv = inverse(conv_real, conv_imag)
    grad_gated = inverse(back_real, back_imag)
    corr = inverse(filter_real, filter_imag)
    grad_filter = lax.psum(corr, "chan") * scale
    grad_q = grad_out * conv
    grad_k = grad_gated * values
    grad_v = grad_gated * k_gate
    return (grad_q, grad_k, grad_v, grad_filter)


def solution(mesh):
    placed = (
        P("seq", "chan"),
        P("seq", "chan"),
        P("seq", "chan"),
        P("seq", None),
        P("seq", "chan"),
    )
    return jax.shard_map(
        local,
        mesh=mesh,
        in_specs=placed,
        out_specs=(P("seq", "chan"), P("seq", "chan"), P("seq", "chan"), P("seq", None)),
        check_vma=False,
    )
```

profile of v0, /device:TPU:32, one launch (start us, length us, event | category | flops | bytes accessed | tf_op | source)
XLA Modules:
  0.0 699.3 jit_solution(10144373009887755012)
XLA Ops:
  8.9 9.7 %all-to-all-start = ((f32[1,512,128]{2,0,1:T(1,128)}), f32[1,512,128]{2,0,1:T(1,128)S(1)}, u32[]{:S(2)}, u32[]{:S(2)}) async-start(f32[1,512,128]{2,0,1:T(1,128)} %bitcast.3), calls=%async_computation | async-start | bytes 524288 | tf_op jit(solution)/shard_map/all_to_all | solution.py:23
  19.9 10.2 %all-to-all-done = f32[1,512,128]{2,0,1:T(1,128)S(1)} async-done(((f32[1,512,128]{2,0,1:T(1,128)}), f32[1,512,128]{2,0,1:T(1,128)S(1)}, u32[]{:S(2)}, u32[]{:S(2)}) %all-to-all-start) | async-done | bytes 262176 | tf_op jit(solution)/shard_map/all_to_all | solution.py:23
  36.1 15.6 %all-to-all-done.3 = f32[1,512,256]{2,0,1:T(1,128)S(1)} async-done(((f32[1,512,256]{2,0,1:T(1,128)}), f32[1,512,256]{2,0,1:T(1,128)S(1)}, u32[]{:S(2)}, u32[]{:S(2)}) %all-to-all-start.3) | async-done | bytes 524320 | tf_op jit(solution)/shard_map/all_to_all | solution.py:23
  59.5 14.1 %all-to-all-done.9 = f32[1,512,256]{2,0,1:T(1,128)S(1)} async-done(((f32[1,512,256]{2,0,1:T(1,128)}), f32[1,512,256]{2,0,1:T(1,128)S(1)}, u32[]{:S(2)}, u32[]{:S(2)}) %all-to-all-start.9) | async-done | bytes 524320 | tf_op jit(solution)/shard_map/all_to_all | solution.py:23
  79.7 15.7 %all-to-all-done.2 = f32[64,16,128]{2,1,0:T(8,128)S(1)} async-done(((f32[64,16,128]{2,1,0:T(8,128)}), f32[64,16,128]{2,1,0:T(8,128)S(1)}, u32[]{:S(2)}, u32[]{:S(2)}) %all-to-all-start.2) | async-done | bytes 524320 | tf_op jit(solution)/shard_map/all_to_all | solution.py:35
  109.2 9.6 %all-to-all-done.1 = f32[64,16,128]{2,1,0:T(8,128)} async-done(((f32[64,16,128]{2,1,0:T(8,128)}), f32[64,16,128]{2,1,0:T(8,128)}, u32[]{:S(2)}, u32[]{:S(2)}) %all-to-all-start.1) | async-done | bytes 524320 | tf_op jit(solution)/shard_map/all_to_all | solution.py:34
  126.3 26.6 %all-to-all-done.10 = f32[64,16,256]{2,1,0:T(8,128)} async-done(((f32[64,16,256]{2,1,0:T(8,128)}), f32[64,16,256]{2,1,0:T(8,128)}, u32[]{:S(2)}, u32[]{:S(2)}) %all-to-all-start.10) | async-done | bytes 1048608 | tf_op jit(solution)/shard_map/all_to_all | solution.py:34
  159.5 26.5 %all-to-all-done.11 = f32[64,16,256]{2,1,0:T(8,128)S(1)} async-done(((f32[64,16,256]{2,1,0:T(8,128)}), f32[64,16,256]{2,1,0:T(8,128)S(1)}, u32[]{:S(2)}, u32[]{:S(2)}) %all-to-all-start.11) | async-done | bytes 1048608 | tf_op jit(solution)/shard_map/all_to_all | solution.py:35
  192.9 26.3 %all-to-all-done.4 = f32[64,16,256]{2,1,0:T(8,128)S(1)} async-done(((f32[64,16,256]{2,1,0:T(8,128)}), f32[64,16,256]{2,1,0:T(8,128)S(1)}, u32[]{:S(2)}, u32[]{:S(2)}) %all-to-all-start.4) | async-done | bytes 1048608 | tf_op jit(solution)/shard_map/all_to_all | solution.py:34
  244.0 6.7 fusion.5
  252.2 7.5 %fusion.38 = f32[2,256,512]{2,1,0:T(8,128)S(1)} fusion(f32[2,512,256]{2,1,0:T(8,128)S(1)} %bitcast.255), kind=kOutput, calls=%fused_computation.67 | convolution fusion | flops 1614282752 | bytes 2097152 | tf_op jit(solution)/shard_map/kn,tnw->tkw/dot_general | solution.py:9
  259.7 8.0 %fusion.48 = f32[2,256,512]{2,1,0:T(8,128)} fusion(f32[2,512,256]{2,1,0:T(8,128)S(1)} %bitcast.238), kind=kOutput, calls=%fused_computation.77 | convolution fusion | flops 1614282752 | bytes 2097152 | tf_op jit(solution)/shard_map/kn,tnw->tkw/dot_general | solution.py:9
  267.7 8.0 %fusion.36 = f32[2,256,512]{2,1,0:T(8,128)} fusion(f32[2,512,256]{2,1,0:T(8,128)S(1)} %bitcast.257), kind=kOutput, calls=%fused_computation.65 | convolution fusion | flops 1614282752 | bytes 2097152 | tf_op jit(solution)/shard_map/kn,tnw->tkw/dot_general | solution.py:9
  275.7 8.2 %fusion.1 = f32[2,512,256]{1,2,0:T(8,128)} fusion(f32[2,256,512]{2,1,0:T(8,128)S(1)} %fusion.38, f32[2,512,256]{2,1,0:T(8,128)S(1)} %bitcast.258), kind=kOutput, calls=%fused_computation.18 | convolution fusion | flops 1614544896 | bytes 3145728 | tf_op jit(solution)/shard_map/kn,tnw->tkw/dot_general | solution.py:9
  285.2 7.5 %fusion.44 = f32[2,256,512]{2,1,0:T(8,128)S(1)} fusion(f32[2,512,256]{2,1,0:T(8,128)S(1)} %bitcast.259), kind=kOutput, calls=%fused_computation.73 | convolution fusion | flops 1614282752 | bytes 2097152 | tf_op jit(solution)/shard_map/kn,tnw->tkw/dot_general | solution.py:9
  292.7 7.6 %fusion.3 = f32[2,512,256]{1,2,0:T(8,128)S(1)} fusion(f32[2,256,512]{2,1,0:T(8,128)S(1)} %copy-done.28, f32[2,512,256]{2,1,0:T(8,128)S(1)} %bitcast.260), kind=kOutput, calls=%fused_computation.24 | convolution fusion | flops 1614544896 | bytes 3145728 | tf_op jit(solution)/shard_map/kn,tnw->tkw/dot_general | solution.py:9
  300.3 7.8 %fusion = f32[2,512,256]{1,2,0:T(8,128)S(1)} fusion(f32[2,256,512]{2,1,0:T(8,128)S(1)} %copy-done.26, f32[2,512,256]{2,1,0:T(8,128)S(1)} %bitcast.256), kind=kOutput, calls=%fused_computation.16 | convolution fusion | flops 1614544896 | bytes 3145728 | tf_op jit(solution)/shard_map/kn,tnw->tkw/dot_general | solution.py:9
  308.2 11.9 %multiply_add_fusion = (f32[2,512,256]{1,2,0:T(8,128)S(1)}, f32[2,512,256]{1,2,0:T(8,128)S(1)}, f32[2,512,256]{1,2,0:T(8,128)}, f32[2,512,256]{1,2,0:T(8,128)}, ...) fusion(f32[2,512,256]{1,2,0:T(8,128)S(1)} %fusion, f32[2,512,256]{1,2,0:T(8,128)S(1)} %fusion.3, ...), kind=kOutput, calls=%fused_computation.82 | convolution fusion | flops 1619263488 | bytes 12582912 | tf_op jit(solution)/shard_map/kn,tnw->tkw/dot_general | solution.py:9
  343.1 8.8 %all-to-all-start.15 = ((f32[2,512,128]{2,0,1:T(2,128)}), f32[2,512,128]{2,0,1:T(2,128)S(1)}, u32[]{:S(2)}, u32[]{:S(2)}) async-start(f32[2,512,128]{2,0,1:T(2,128)} %copy.151), calls=%async_computation.15 | async-start | bytes 1048576 | tf_op jit(solution)/shard_map/all_to_all | solution.py:64
  359.2 6.7 fusion.34
  365.9 6.7 convolution_add_fusion
  372.6 8.7 %all-to-all-start.16 = ((f32[2,512,128]{2,0,1:T(2,128)}), f32[2,512,128]{2,0,1:T(2,128)S(1)}, u32[]{:S(2)}, u32[]{:S(2)}) async-start(f32[2,512,128]{2,0,1:T(2,128)} %copy.154), calls=%async_computation.16 | async-start | bytes 1048576 | tf_op jit(solution)/shard_map/all_to_all | solution.py:65
  394.4 6.7 convolution_add_fusion.2
  403.8 8.8 %all-to-all-start.17 = ((f32[32,16,128]{2,1,0:T(8,128)}), f32[32,16,128]{2,1,0:T(8,128)S(1)}, u32[]{:S(2)}, u32[]{:S(2)}) async-start(f32[32,16,128]{2,1,0:T(8,128)} %copy.157), calls=%async_computation.17 | async-start | bytes 524288 | tf_op jit(solution)/shard_map/all_to_all | solution.py:74
  419.0 7.3 %add_bitcast_fusion = (f32[2,512,256]{1,2,0:T(8,128)}, f32[2,512,256]{1,2,0:T(8,128)S(1)}, f32[2,512,256]{1,2,0:T(8,128)}, f32[2,512,256]{1,2,0:T(8,128)S(1)}) fusion(f32[2,256,512]{2,1,0:T(8,128)S(1)} %copy-done.21, f32[2,256,512]{2,1,0:T(8,128)S(1)} %copy-done.20, f32[2,512]{1,0:T(2,128)S(1)} %get-tuple-element.33, f32[2,512]{1,0:T(2,128)S(1)} %get-tuple-element.32, ...), kind=kOutput, calls=%fused_computation.83 | convolution fusion | flops 1617690624 | bytes 9445376 | tf_op jit(solution)/shard_map/nk,tkw->tnw/dot_general | solution.py:9
  428.3 8.3 %all-to-all-start.12 = ((f32[2,512,256]{2,0,1:T(2,128)}), f32[2,512,256]{2,0,1:T(2,128)S(1)}, u32[]{:S(2)}, u32[]{:S(2)}) async-start(f32[2,512,256]{2,0,1:T(2,128)} %copy.144), calls=%async_computation.12 | async-start | bytes 2097152 | tf_op jit(solution)/shard_map/all_to_all | solution.py:64
  437.9 26.7 %all-to-all-done.12 = f32[2,512,256]{2,0,1:T(2,128)S(1)} async-done(((f32[2,512,256]{2,0,1:T(2,128)}), f32[2,512,256]{2,0,1:T(2,128)S(1)}, u32[]{:S(2)}, u32[]{:S(2)}) %all-to-all-start.12) | async-done | bytes 1048608 | tf_op jit(solution)/shard_map/all_to_all | solution.py:64
  471.3 25.8 %all-to-all-done.13 = f32[2,512,256]{2,0,1:T(2,128)S(1)} async-done(((f32[2,512,256]{2,0,1:T(2,128)}), f32[2,512,256]{2,0,1:T(2,128)S(1)}, u32[]{:S(2)}, u32[]{:S(2)}) %all-to-all-start.13) | async-done | bytes 1048608 | tf_op jit(solution)/shard_map/all_to_all | solution.py:65
  504.5 26.8 %all-to-all-done.6 = f32[2,512,256]{2,0,1:T(2,128)S(1)} async-done(((f32[2,512,256]{2,0,1:T(2,128)}), f32[2,512,256]{2,0,1:T(2,128)S(1)}, u32[]{:S(2)}, u32[]{:S(2)}) %all-to-all-start.6) | async-done | bytes 1048608 | tf_op jit(solution)/shard_map/all_to_all | solution.py:64
  549.4 15.2 %all-to-all-done.7 = f32[2,512,256]{2,0,1:T(2,128)S(1)} async-done(((f32[2,512,256]{2,0,1:T(2,128)}), f32[2,512,256]{2,0,1:T(2,128)S(1)}, u32[]{:S(2)}, u32[]{:S(2)}) %all-to-all-start.7) | async-done | bytes 1048608 | tf_op jit(solution)/shard_map/all_to_all | solution.py:65
  576.0 11.2 %all-to-all-done.14 = f32[32,16,256]{2,1,0:T(8,128)} async-done(((f32[32,16,256]{2,1,0:T(8,128)}), f32[32,16,256]{2,1,0:T(8,128)}, u32[]{:S(2)}, u32[]{:S(2)}) %all-to-all-start.14) | async-done | bytes 524320 | tf_op jit(solution)/shard_map/all_to_all | solution.py:74
  593.1 94.4 %all-reduce.2.cloned.1.call-done = f32[512,128]{1,0:T(8,128)} async-done(((f32[512,128]{1,0:T(8,128)}), f32[512,128]{1,0:T(8,128)}) %all-reduce.2.cloned.1.call-update) | async-done | bytes 262160 | tf_op jit(solution)/shard_map/psum | solution.py:121
  (154 shorter events, 194.7 us)
Async XLA Ops:
  7.2 11.4 %copy-start.6 = (f32[512,256]{1,0:T(8,128)S(1)}, f32[512,256]{1,0:T(8,128)}, u32[]{:S(2)}) copy-start(f32[512,256]{1,0:T(8,128)} %param.6) | copy-start | bytes 1572868
  7.2 11.4 %copy-start.8 = (f32[512,256]{1,0:T(8,128)S(1)}, f32[512,256]{1,0:T(8,128)}, u32[]{:S(2)}) copy-start(f32[512,256]{1,0:T(8,128)} %param.7) | copy-start | bytes 1572868
  8.9 21.1 %all-to-all-start = ((f32[1,512,128]{2,0,1:T(1,128)}), f32[1,512,128]{2,0,1:T(1,128)S(1)}, u32[]{:S(2)}, u32[]{:S(2)}) async-start(f32[1,512,128]{2,0,1:T(1,128)} %bitcast.3), calls=%async_computation | async-start | bytes 524288 | tf_op jit(solution)/shard_map/all_to_all | solution.py:23
  19.9 14.9 %copy-start.10 = (f32[512,256]{1,0:T(8,128)S(1)}, f32[512,256]{1,0:T(8,128)}, u32[]{:S(2)}) copy-start(f32[512,256]{1,0:T(8,128)} %param.9) | copy-start | bytes 1572868
  19.9 14.9 %copy-start.23 = (f32[512,256]{1,0:T(8,128)S(1)}, f32[512,256]{1,0:T(8,128)}, u32[]{:S(2)}) copy-start(f32[512,256]{1,0:T(8,128)} %param.5) | copy-start | bytes 1572868
  30.0 21.6 %all-to-all-start.3 = ((f32[1,512,256]{2,0,1:T(1,128)}), f32[1,512,256]{2,0,1:T(1,128)S(1)}, u32[]{:S(2)}, u32[]{:S(2)}) async-start(f32[1,512,256]{2,0,1:T(1,128)} %broadcast_in_dim.7), calls=%async_computation.3 | async-start | bytes 1048576 | tf_op jit(solution)/shard_map/all_to_all | solution.py:23
  51.7 21.9 %all-to-all-start.9 = ((f32[1,512,256]{2,0,1:T(1,128)}), f32[1,512,256]{2,0,1:T(1,128)S(1)}, u32[]{:S(2)}, u32[]{:S(2)}) async-start(f32[1,512,256]{2,0,1:T(1,128)} %broadcast_in_dim.8), calls=%async_computation.9 | async-start | bytes 1048576 | tf_op jit(solution)/shard_map/all_to_all | solution.py:23
  73.6 21.9 %all-to-all-start.2 = ((f32[64,16,128]{2,1,0:T(8,128)}), f32[64,16,128]{2,1,0:T(8,128)S(1)}, u32[]{:S(2)}, u32[]{:S(2)}) async-start(f32[64,16,128]{2,1,0:T(8,128)} %copy.112), calls=%async_computation.2 | async-start | bytes 1048576 | tf_op jit(solution)/shard_map/all_to_all | solution.py:35
  96.3 22.6 %all-to-all-start.1 = ((f32[64,16,128]{2,1,0:T(8,128)}), f32[64,16,128]{2,1,0:T(8,128)}, u32[]{:S(2)}, u32[]{:S(2)}) async-start(f32[64,16,128]{2,1,0:T(8,128)} %copy.109), calls=%async_computation.1 | async-start | bytes 1048576 | tf_op jit(solution)/shard_map/all_to_all | solution.py:34
  118.9 34.1 %all-to-all-start.10 = ((f32[64,16,256]{2,1,0:T(8,128)}), f32[64,16,256]{2,1,0:T(8,128)}, u32[]{:S(2)}, u32[]{:S(2)}) async-start(f32[64,16,256]{2,1,0:T(8,128)} %copy.136), calls=%async_computation.10 | async-start | bytes 2097152 | tf_op jit(solution)/shard_map/all_to_all | solution.py:34
  152.9 33.1 %all-to-all-start.11 = ((f32[64,16,256]{2,1,0:T(8,128)}), f32[64,16,256]{2,1,0:T(8,128)S(1)}, u32[]{:S(2)}, u32[]{:S(2)}) async-start(f32[64,16,256]{2,1,0:T(8,128)} %copy.139), calls=%async_computation.11 | async-start | bytes 2097152 | tf_op jit(solution)/shard_map/all_to_all | solution.py:35
  186.0 33.1 %all-to-all-start.4 = ((f32[64,16,256]{2,1,0:T(8,128)}), f32[64,16,256]{2,1,0:T(8,128)S(1)}, u32[]{:S(2)}, u32[]{:S(2)}) async-start(f32[64,16,256]{2,1,0:T(8,128)} %copy.117), calls=%async_computation.4 | async-start | bytes 2097152 | tf_op jit(solution)/shard_map/all_to_all | solution.py:34
  219.2 64.7 %all-to-all-start.5 = ((f32[64,16,256]{2,1,0:T(8,128)}), f32[64,16,256]{2,1,0:T(8,128)}, u32[]{:S(2)}, u32[]{:S(2)}) async-start(f32[64,16,256]{2,1,0:T(8,128)} %copy.120), calls=%async_computation.5 | async-start | bytes 2097152 | tf_op jit(solution)/shard_map/all_to_all | solution.py:35
  292.7 7.6 %copy-start.26 = (f32[2,256,512]{2,1,0:T(8,128)S(1)}, f32[2,256,512]{2,1,0:T(8,128)}, u32[]{:S(2)}) copy-start(f32[2,256,512]{2,1,0:T(8,128)} %fusion.36) | copy-start | bytes 3145732
  300.3 7.8 %copy-start.18 = (f32[2,512,256]{1,2,0:T(8,128)S(1)}, f32[2,512,256]{1,2,0:T(8,128)}, u32[]{:S(2)}) copy-start(f32[2,512,256]{1,2,0:T(8,128)} %fusion.1) | copy-start | bytes 3145732
  300.3 7.8 %copy-start.24 = (f32[2,512,128]{1,2,0:T(8,128)S(1)}, f32[2,512,128]{1,2,0:T(8,128)}, u32[]{:S(2)}) copy-start(f32[2,512,128]{1,2,0:T(8,128)} %fusion.4) | copy-start | bytes 1572868
  300.3 7.8 %copy-start.25 = (f32[2,512,128]{1,2,0:T(8,128)S(1)}, f32[2,512,128]{1,2,0:T(8,128)}, u32[]{:S(2)}) copy-start(f32[2,512,128]{1,2,0:T(8,128)} %fusion.5) | copy-start | bytes 1572868
  343.1 9.8 %copy-start.15 = (f32[2,512,256]{1,2,0:T(8,128)S(1)}, f32[2,512,256]{1,2,0:T(8,128)}, u32[]{:S(2)}) copy-start(f32[2,512,256]{1,2,0:T(8,128)} %get-tuple-element.18) | copy-start | bytes 3145732
  343.1 29.5 %all-to-all-start.15 = ((f32[2,512,128]{2,0,1:T(2,128)}), f32[2,512,128]{2,0,1:T(2,128)S(1)}, u32[]{:S(2)}, u32[]{:S(2)}) async-start(f32[2,512,128]{2,0,1:T(2,128)} %copy.151), calls=%async_computation.15 | async-start | bytes 1048576 | tf_op jit(solution)/shard_map/all_to_all | solution.py:64
  372.6 8.7 %copy-start.4 = (f32[2,512,256]{1,2,0:T(8,128)S(1)}, f32[2,512,256]{1,2,0:T(8,128)}, u32[]{:S(2)}) copy-start(f32[2,512,256]{1,2,0:T(8,128)} %get-tuple-element.20) | copy-start | bytes 3145732
  372.6 29.5 %all-to-all-start.16 = ((f32[2,512,128]{2,0,1:T(2,128)}), f32[2,512,128]{2,0,1:T(2,128)S(1)}, u32[]{:S(2)}, u32[]{:S(2)}) async-start(f32[2,512,128]{2,0,1:T(2,128)} %copy.154), calls=%async_computation.16 | async-start | bytes 1048576 | tf_op jit(solution)/shard_map/all_to_all | solution.py:65
  403.8 23.8 %all-to-all-start.17 = ((f32[32,16,128]{2,1,0:T(8,128)}), f32[32,16,128]{2,1,0:T(8,128)S(1)}, u32[]{:S(2)}, u32[]{:S(2)}) async-start(f32[32,16,128]{2,1,0:T(8,128)} %copy.157), calls=%async_computation.17 | async-start | bytes 524288 | tf_op jit(solution)/shard_map/all_to_all | solution.py:74
  427.6 9.0 %copy-start.5 = (f32[2,512,256]{1,2,0:T(8,128)S(1)}, f32[2,512,256]{1,2,0:T(8,128)}, u32[]{:S(2)}) copy-start(f32[2,512,256]{1,2,0:T(8,128)} %get-tuple-element.14) | copy-start | bytes 3145732
  428.3 36.3 %all-to-all-start.12 = ((f32[2,512,256]{2,0,1:T(2,128)}), f32[2,512,256]{2,0,1:T(2,128)S(1)}, u32[]{:S(2)}, u32[]{:S(2)}) async-start(f32[2,512,256]{2,0,1:T(2,128)} %copy.144), calls=%async_computation.12 | async-start | bytes 2097152 | tf_op jit(solution)/shard_map/all_to_all | solution.py:64
  464.6 32.5 %all-to-all-start.13 = ((f32[2,512,256]{2,0,1:T(2,128)}), f32[2,512,256]{2,0,1:T(2,128)S(1)}, u32[]{:S(2)}, u32[]{:S(2)}) async-start(f32[2,512,256]{2,0,1:T(2,128)} %copy.147), calls=%async_computation.13 | async-start | bytes 2097152 | tf_op jit(solution)/shard_map/all_to_all | solution.py:65
  498.2 33.1 %all-to-all-start.6 = ((f32[2,512,256]{2,0,1:T(2,128)}), f32[2,512,256]{2,0,1:T(2,128)S(1)}, u32[]{:S(2)}, u32[]{:S(2)}) async-start(f32[2,512,256]{2,0,1:T(2,128)} %copy.127), calls=%async_computation.6 | async-start | bytes 2097152 | tf_op jit(solution)/shard_map/all_to_all | solution.py:64
  531.3 33.3 %all-to-all-start.7 = ((f32[2,512,256]{2,0,1:T(2,128)}), f32[2,512,256]{2,0,1:T(2,128)S(1)}, u32[]{:S(2)}, u32[]{:S(2)}) async-start(f32[2,512,256]{2,0,1:T(2,128)} %copy.130), calls=%async_computation.7 | async-start | bytes 2097152 | tf_op jit(solution)/shard_map/all_to_all | solution.py:65
  564.6 22.6 %all-to-all-start.14 = ((f32[32,16,256]{2,1,0:T(8,128)}), f32[32,16,256]{2,1,0:T(8,128)}, u32[]{:S(2)}, u32[]{:S(2)}) async-start(f32[32,16,256]{2,1,0:T(8,128)} %copy.150), calls=%async_computation.14 | async-start | bytes 1048576 | tf_op jit(solution)/shard_map/all_to_all | solution.py:74
  587.2 102.0 %copy-start.9 = (f32[512,256]{1,0:T(8,128)S(1)}, f32[512,256]{1,0:T(8,128)}, u32[]{:S(2)}) copy-start(f32[512,256]{1,0:T(8,128)} %param.7) | copy-start | bytes 1572868
  587.2 104.2 %all-to-all-start.8 = ((f32[32,16,256]{2,1,0:T(8,128)}), f32[32,16,256]{2,1,0:T(8,128)S(1)}, u32[]{:S(2)}, u32[]{:S(2)}) async-start(f32[32,16,256]{2,1,0:T(8,128)} %copy.133), calls=%async_computation.8 | async-start | bytes 1048576 | tf_op jit(solution)/shard_map/all_to_all | solution.py:74
  592.3 96.9 %copy-start.7 = (f32[512,256]{1,0:T(8,128)S(1)}, f32[512,256]{1,0:T(8,128)}, u32[]{:S(2)}) copy-start(f32[512,256]{1,0:T(8,128)} %param.6) | copy-start | bytes 1572868
  592.3 95.2 %all-reduce.2.cloned.1.call-start = ((), (), s32[]{:S(2)}) async-start(), calls=%async_computation.18 | async-start | bytes 524288 | tf_op jit(solution)/shard_map/psum | solution.py:121
  (16 other events, 66.0 us)
Sparse Core Ops, SparseCore 0:
  596.3 91.1 all-reduce.1
where the time goes:
time: 710 us; the launch traced here: 699 us
  waiting for transfers between devices  345 us (49%)
  matrix products  177 us (25%)
  starting transfers between devices  112 us (16%)
  local copies, waits for them, and re-layouts  43.1 us (6%)
  between operations  15.1 us (2%)
    dot_general x36, matrix products, product_hi(): return jnp.einsum(form, left, right, precision=lax.Precision.HIGHEST)  177 us
    psum x1, waiting for transfers between devices, local(): grad_filter = lax.psum(corr, 'chan') * scale  94.4 us
    all_to_all x3, waiting for transfers between devices, forward_transform(): lax.all_to_all(turned_real, 'seq', split_axis=0, concat_axis=1, tiled=True)  62.5 us
    all_to_all x3, waiting for transfers between devices, inverse_transform(): lax.all_to_all(turned_real, 'seq', split_axis=1, concat_axis=0, tiled=True)  53.5 us
    all_to_all x3, waiting for transfers between devices, forward_transform(): lax.all_to_all(turned_imag, 'seq', split_axis=0, concat_axis=1, tiled=True)  42.3 us
    all_to_all x3, waiting for transfers between devices, inverse_transform(): lax.all_to_all(turned_imag, 'seq', split_axis=1, concat_axis=0, tiled=True)  41 us
    all_to_all x3, waiting for transfers between devices, forward_transform(): lax.all_to_all(block[None], 'seq', split_axis=1, concat_axis=0, tiled=True)  39.9 us
    all_to_all x3, starting transfers between devices, inverse_transform(): lax.all_to_all(turned_real, 'seq', split_axis=1, concat_axis=0, tiled=True)  22 us
  transfers between devices with their start and end apart: 19, of which 14 were waited for; matrix products, arithmetic and copies ran while one was open for 22% of the time, Pallas kernels for 0%

commit v1 on v0

--- a/solution.py
+++ b/solution.py
@@ -118,7 +118,7 @@
     conv = inverse(conv_real, conv_imag)
     grad_gated = inverse(back_real, back_imag)
     corr = inverse(filter_real, filter_imag)
-    grad_filter = lax.psum(corr, "chan") * scale
+    grad_filter = jnp.sum(lax.all_gather(corr, "chan"), axis=0) * scale
     grad_q = grad_out * conv
     grad_k = grad_gated * values
     grad_v = grad_gated * k_gate

time: 710 us -> 631 us (0.89)
  waiting for transfers between devices: 345 us -> 263 us
    psum x1 -> x0, waiting for transfers between devices: 94.4 us -> none  [local(): grad_filter = lax.psum(corr, 'chan') * scale]
    all_to_all x3, waiting for transfers between devices: 11.2 us -> 26.1 us  [inverse_transform(): lax.all_to_all(spatial, 'seq', split_axis=0, concat_axis=1, tiled=True)]
  transfers between devices with their start and end apart: 19 -> 19, of which waited for: 14 -> 14; matrix products, arithmetic and copies ran while one was open for 22% -> 25% of each run, Pallas kernels for 0% -> 0%
where the time goes in v1:
time: 631 us; the launch traced here: 619 us
  waiting for transfers between devices  263 us (42%)
  matrix products  178 us (28%)
  starting transfers between devices  111 us (18%)
  local copies, waits for them, and re-layouts  42.8 us (7%)
  between operations  15.1 us (2%)
  other arithmetic  8.91 us (1%)
    dot_general x36, matrix products, product_hi(): return jnp.einsum(form, left, right, precision=lax.Precision.HIGHEST)  178 us
    all_to_all x3, waiting for transfers between devices, forward_transform(): lax.all_to_all(turned_real, 'seq', split_axis=0, concat_axis=1, tiled=True)  61.7 us
    all_to_all x3, waiting for transfers between devices, inverse_transform(): lax.all_to_all(turned_real, 'seq', split_axis=1, concat_axis=0, tiled=True)  53.5 us
    all_to_all x3, waiting for transfers between devices, forward_transform(): lax.all_to_all(turned_imag, 'seq', split_axis=0, concat_axis=1, tiled=True)  42.3 us
    all_to_all x3, waiting for transfers between devices, inverse_transform(): lax.all_to_all(turned_imag, 'seq', split_axis=1, concat_axis=0, tiled=True)  40.5 us
    all_to_all x3, waiting for transfers between devices, forward_transform(): lax.all_to_all(block[None], 'seq', split_axis=1, concat_axis=0, tiled=True)  38.7 us
    all_to_all x3, waiting for transfers between devices, inverse_transform(): lax.all_to_all(spatial, 'seq', split_axis=0, concat_axis=1, tiled=True)  26.1 us
    all_to_all x3, starting transfers between devices, inverse_transform(): lax.all_to_all(turned_real, 'seq', split_axis=1, concat_axis=0, tiled=True)  21.3 us
  transfers between devices with their start and end apart: 19, of which 14 were waited for; matrix products, arithmetic and copies ran while one was open for 25% of the time, Pallas kernels for 0%

profile of v1, /device:TPU:32, one launch (start us, length us, event | category | flops | bytes accessed | tf_op | source)
XLA Modules:
  0.0 618.9 jit_solution(6255386853611010709)
XLA Ops:
  8.8 9.8 %all-to-all-start = ((f32[1,512,128]{2,0,1:T(1,128)}), f32[1,512,128]{2,0,1:T(1,128)S(1)}, u32[]{:S(2)}, u32[]{:S(2)}) async-start(f32[1,512,128]{2,0,1:T(1,128)} %bitcast.2), calls=%async_computation | async-start | bytes 524288 | tf_op jit(solution)/shard_map/all_to_all | solution.py:23
  21.1 9.0 %all-to-all-done = f32[1,512,128]{2,0,1:T(1,128)S(1)} async-done(((f32[1,512,128]{2,0,1:T(1,128)}), f32[1,512,128]{2,0,1:T(1,128)S(1)}, u32[]{:S(2)}, u32[]{:S(2)}) %all-to-all-start) | async-done | bytes 262176 | tf_op jit(solution)/shard_map/all_to_all | solution.py:23
  36.1 15.6 %all-to-all-done.3 = f32[1,512,256]{2,0,1:T(1,128)S(1)} async-done(((f32[1,512,256]{2,0,1:T(1,128)}), f32[1,512,256]{2,0,1:T(1,128)S(1)}, u32[]{:S(2)}, u32[]{:S(2)}) %all-to-all-start.3) | async-done | bytes 524320 | tf_op jit(solution)/shard_map/all_to_all | solution.py:23
  59.5 14.1 %all-to-all-done.9 = f32[1,512,256]{2,0,1:T(1,128)S(1)} async-done(((f32[1,512,256]{2,0,1:T(1,128)}), f32[1,512,256]{2,0,1:T(1,128)S(1)}, u32[]{:S(2)}, u32[]{:S(2)}) %all-to-all-start.9) | async-done | bytes 524320 | tf_op jit(solution)/shard_map/all_to_all | solution.py:23
  79.7 15.7 %all-to-all-done.2 = f32[64,16,128]{2,1,0:T(8,128)S(1)} async-done(((f32[64,16,128]{2,1,0:T(8,128)}), f32[64,16,128]{2,1,0:T(8,128)S(1)}, u32[]{:S(2)}, u32[]{:S(2)}) %all-to-all-start.2) | async-done | bytes 524320 | tf_op jit(solution)/shard_map/all_to_all | solution.py:35
  108.4 9.6 %all-to-all-done.1 = f32[64,16,128]{2,1,0:T(8,128)} async-done(((f32[64,16,128]{2,1,0:T(8,128)}), f32[64,16,128]{2,1,0:T(8,128)}, u32[]{:S(2)}, u32[]{:S(2)}) %all-to-all-start.1) | async-done | bytes 524320 | tf_op jit(solution)/shard_map/all_to_all | solution.py:34
  125.6 26.6 %all-to-all-done.10 = f32[64,16,256]{2,1,0:T(8,128)} async-done(((f32[64,16,256]{2,1,0:T(8,128)}), f32[64,16,256]{2,1,0:T(8,128)}, u32[]{:S(2)}, u32[]{:S(2)}) %all-to-all-start.10) | async-done | bytes 1048608 | tf_op jit(solution)/shard_map/all_to_all | solution.py:34
  158.8 26.5 %all-to-all-done.11 = f32[64,16,256]{2,1,0:T(8,128)S(1)} async-done(((f32[64,16,256]{2,1,0:T(8,128)}), f32[64,16,256]{2,1,0:T(8,128)S(1)}, u32[]{:S(2)}, u32[]{:S(2)}) %all-to-all-start.11) | async-done | bytes 1048608 | tf_op jit(solution)/shard_map/all_to_all | solution.py:35
  192.9 25.5 %all-to-all-done.4 = f32[64,16,256]{2,1,0:T(8,128)S(1)} async-done(((f32[64,16,256]{2,1,0:T(8,128)}), f32[64,16,256]{2,1,0:T(8,128)S(1)}, u32[]{:S(2)}, u32[]{:S(2)}) %all-to-all-start.4) | async-done | bytes 1048608 | tf_op jit(solution)/shard_map/all_to_all | solution.py:34
  243.4 6.8 %fusion.5 = f32[2,512,128]{1,2,0:T(8,128)} fusion(f32[2,128,512]{2,1,0:T(8,128)S(1)} %fusion.50, f32[2,512,128]{2,1,0:T(8,128)S(1)} %bitcast.262), kind=kOutput, calls=%fused_computation.30 | convolution fusion | flops 809107456 | bytes 1572864 | tf_op jit(solution)/shard_map/kn,tnw->tkw/dot_general | solution.py:9
  252.5 7.5 %fusion.38 = f32[2,256,512]{2,1,0:T(8,128)S(1)} fusion(f32[2,512,256]{2,1,0:T(8,128)S(1)} %bitcast.254), kind=kOutput, calls=%fused_computation.67 | convolution fusion | flops 1614282752 | bytes 2097152 | tf_op jit(solution)/shard_map/kn,tnw->tkw/dot_general | solution.py:9
  260.0 8.0 %fusion.48 = f32[2,256,512]{2,1,0:T(8,128)} fusion(f32[2,512,256]{2,1,0:T(8,128)S(1)} %bitcast.236), kind=kOutput, calls=%fused_computation.77 | convolution fusion | flops 1614282752 | bytes 2097152 | tf_op jit(solution)/shard_map/kn,tnw->tkw/dot_general | solution.py:9
  268.0 8.1 %fusion.36 = f32[2,256,512]{2,1,0:T(8,128)} fusion(f32[2,512,256]{2,1,0:T(8,128)S(1)} %bitcast.256), kind=kOutput, calls=%fused_computation.65 | convolution fusion | flops 1614282752 | bytes 2097152 | tf_op jit(solution)/shard_map/kn,tnw->tkw/dot_general | solution.py:9
  276.1 8.0 %fusion.1 = f32[2,512,256]{1,2,0:T(8,128)} fusion(f32[2,256,512]{2,1,0:T(8,128)S(1)} %fusion.38, f32[2,512,256]{2,1,0:T(8,128)S(1)} %bitcast.257), kind=kOutput, calls=%fused_computation.18 | convolution fusion | flops 1614544896 | bytes 3145728 | tf_op jit(solution)/shard_map/kn,tnw->tkw/dot_general | solution.py:9
  284.2 7.5 %fusion.44 = f32[2,256,512]{2,1,0:T(8,128)S(1)} fusion(f32[2,512,256]{2,1,0:T(8,128)S(1)} %bitcast.258), kind=kOutput, calls=%fused_computation.73 | convolution fusion | flops 1614282752 | bytes 2097152 | tf_op jit(solution)/shard_map/kn,tnw->tkw/dot_general | solution.py:9
  291.7 7.8 %fusion.3 = f32[2,512,256]{1,2,0:T(8,128)S(1)} fusion(f32[2,256,512]{2,1,0:T(8,128)S(1)} %copy-done.28, f32[2,512,256]{2,1,0:T(8,128)S(1)} %bitcast.259), kind=kOutput, calls=%fused_computation.24 | convolution fusion | flops 1614544896 | bytes 3145728 | tf_op jit(solution)/shard_map/kn,tnw->tkw/dot_general | solution.py:9
  299.6 7.6 %fusion = f32[2,512,256]{1,2,0:T(8,128)S(1)} fusion(f32[2,256,512]{2,1,0:T(8,128)S(1)} %copy-done.26, f32[2,512,256]{2,1,0:T(8,128)S(1)} %bitcast.255), kind=kOutput, calls=%fused_computation.16 | convolution fusion | flops 1614544896 | bytes 3145728 | tf_op jit(solution)/shard_map/kn,tnw->tkw/dot_general | solution.py:9
  307.2 11.9 %multiply_add_fusion = (f32[2,512,256]{1,2,0:T(8,128)S(1)}, f32[2,512,256]{1,2,0:T(8,128)S(1)}, f32[2,512,256]{1,2,0:T(8,128)}, f32[2,512,256]{1,2,0:T(8,128)}, ...) fusion(f32[2,512,256]{1,2,0:T(8,128)S(1)} %fusion, f32[2,512,256]{1,2,0:T(8,128)S(1)} %fusion.3, ...), kind=kOutput, calls=%fused_computation.82 | convolution fusion | flops 1619263488 | bytes 12582912 | tf_op jit(solution)/shard_map/kn,tnw->tkw/dot_general | solution.py:9
  342.6 8.6 %all-to-all-start.15 = ((f32[2,512,128]{2,0,1:T(2,128)}), f32[2,512,128]{2,0,1:T(2,128)S(1)}, u32[]{:S(2)}, u32[]{:S(2)}) async-start(f32[2,512,128]{2,0,1:T(2,128)} %copy.149), calls=%async_computation.15 | async-start | bytes 1048576 | tf_op jit(solution)/shard_map/all_to_all | solution.py:64
  358.5 6.7 %fusion.34 = f32[2,256,512]{2,1,0:T(8,128)} fusion(f32[2,512,256]{1,2,0:T(8,128)S(1)} %copy-done.14), kind=kOutput, calls=%fused_computation.63 | convolution fusion | flops 1614282752 | bytes 2097152 | tf_op jit(solution)/shard_map/nk,tkw->tnw/dot_general | solution.py:9
  365.3 6.7 %convolution_add_fusion = f32[2,256,512]{2,1,0:T(8,128)} fusion(f32[2,256,512]{2,1,0:T(8,128)S(1)} %fusion.32, f32[2,512,256]{1,2,0:T(8,128)S(1)} %copy-done.14), kind=kOutput, calls=%fused_computation.13 | convolution fusion | flops 1614544896 | bytes 3145728 | tf_op jit(solution)/shard_map/nk,tkw->tnw/dot_general | solution.py:9
  372.0 8.6 %all-to-all-start.16 = ((f32[2,512,128]{2,0,1:T(2,128)}), f32[2,512,128]{2,0,1:T(2,128)S(1)}, u32[]{:S(2)}, u32[]{:S(2)}) async-start(f32[2,512,128]{2,0,1:T(2,128)} %copy.152), calls=%async_computation.16 | async-start | bytes 1048576 | tf_op jit(solution)/shard_map/all_to_all | solution.py:65
  393.7 6.7 %convolution_add_fusion.2 = f32[2,256,512]{2,1,0:T(8,128)} fusion(f32[2,256,512]{2,1,0:T(8,128)S(1)} %fusion.40, f32[2,512,256]{1,2,0:T(8,128)S(1)} %copy-done.11), kind=kOutput, calls=%fused_computation.19 | convolution fusion | flops 1614544896 | bytes 3145728 | tf_op jit(solution)/shard_map/nk,tkw->tnw/dot_general | solution.py:9
  403.1 8.8 %all-to-all-start.17 = ((f32[32,16,128]{2,1,0:T(8,128)}), f32[32,16,128]{2,1,0:T(8,128)S(1)}, u32[]{:S(2)}, u32[]{:S(2)}) async-start(f32[32,16,128]{2,1,0:T(8,128)} %copy.155), calls=%async_computation.17 | async-start | bytes 524288 | tf_op jit(solution)/shard_map/all_to_all | solution.py:74
  418.3 7.2 %add_bitcast_fusion = (f32[2,512,256]{1,2,0:T(8,128)}, f32[2,512,256]{1,2,0:T(8,128)}, f32[2,512,256]{1,2,0:T(8,128)S(1)}, f32[2,512,256]{1,2,0:T(8,128)S(1)}) fusion(f32[2,256,512]{2,1,0:T(8,128)S(1)} %copy-done.20, f32[2,256,512]{2,1,0:T(8,128)S(1)} %copy-done.19, f32[2,512]{1,0:T(2,128)S(1)} %get-tuple-element.33, f32[2,512]{1,0:T(2,128)S(1)} %get-tuple-element.32, ...), kind=kOutput, calls=%fused_computation.83 | convolution fusion | flops 1617690624 | bytes 9445376 | tf_op jit(solution)/shard_map/nk,tkw->tnw/dot_general | solution.py:9
  427.8 8.3 %all-to-all-start.12 = ((f32[2,512,256]{2,0,1:T(2,128)}), f32[2,512,256]{2,0,1:T(2,128)S(1)}, u32[]{:S(2)}, u32[]{:S(2)}) async-start(f32[2,512,256]{2,0,1:T(2,128)} %copy.142), calls=%async_computation.12 | async-start | bytes 2097152 | tf_op jit(solution)/shard_map/all_to_all | solution.py:64
  437.4 26.7 %all-to-all-done.12 = f32[2,512,256]{2,0,1:T(2,128)S(1)} async-done(((f32[2,512,256]{2,0,1:T(2,128)}), f32[2,512,256]{2,0,1:T(2,128)S(1)}, u32[]{:S(2)}, u32[]{:S(2)}) %all-to-all-start.12) | async-done | bytes 1048608 | tf_op jit(solution)/shard_map/all_to_all | solution.py:64
  469.8 26.8 %all-to-all-done.6 = f32[2,512,256]{2,0,1:T(2,128)S(1)} async-done(((f32[2,512,256]{2,0,1:T(2,128)}), f32[2,512,256]{2,0,1:T(2,128)S(1)}, u32[]{:S(2)}, u32[]{:S(2)}) %all-to-all-start.6) | async-done | bytes 1048608 | tf_op jit(solution)/shard_map/all_to_all | solution.py:64
  503.9 25.9 %all-to-all-done.7 = f32[2,512,256]{2,0,1:T(2,128)S(1)} async-done(((f32[2,512,256]{2,0,1:T(2,128)}), f32[2,512,256]{2,0,1:T(2,128)S(1)}, u32[]{:S(2)}, u32[]{:S(2)}) %all-to-all-start.7) | async-done | bytes 1048608 | tf_op jit(solution)/shard_map/all_to_all | solution.py:65
  549.3 14.7 %all-to-all-done.13 = f32[2,512,256]{2,0,1:T(2,128)S(1)} async-done(((f32[2,512,256]{2,0,1:T(2,128)}), f32[2,512,256]{2,0,1:T(2,128)S(1)}, u32[]{:S(2)}, u32[]{:S(2)}) %all-to-all-start.13) | async-done | bytes 1048608 | tf_op jit(solution)/shard_map/all_to_all | solution.py:65
  575.4 11.1 %all-to-all-done.8 = f32[32,16,256]{2,1,0:T(8,128)} async-done(((f32[32,16,256]{2,1,0:T(8,128)}), f32[32,16,256]{2,1,0:T(8,128)}, u32[]{:S(2)}, u32[]{:S(2)}) %all-to-all-start.8) | async-done | bytes 524320 | tf_op jit(solution)/shard_map/all_to_all | solution.py:74
  593.4 15.0 %all-to-all-done.14 = f32[32,16,256]{2,1,0:T(8,128)S(1)} async-done(((f32[32,16,256]{2,1,0:T(8,128)}), f32[32,16,256]{2,1,0:T(8,128)S(1)}, u32[]{:S(2)}, u32[]{:S(2)}) %all-to-all-start.14) | async-done | bytes 524320 | tf_op jit(solution)/shard_map/all_to_all | solution.py:74
  (157 shorter events, 196.4 us)
Async XLA Ops:
  8.8 26.0 %copy-start.5 = (f32[512,256]{1,0:T(8,128)S(1)}, f32[512,256]{1,0:T(8,128)}, u32[]{:S(2)}) copy-start(f32[512,256]{1,0:T(8,128)} %param.9) | copy-start | bytes 1572868
  8.8 26.0 %copy-start.22 = (f32[512,256]{1,0:T(8,128)S(1)}, f32[512,256]{1,0:T(8,128)}, u32[]{:S(2)}) copy-start(f32[512,256]{1,0:T(8,128)} %param.5) | copy-start | bytes 1572868
  8.8 21.2 %all-to-all-start = ((f32[1,512,128]{2,0,1:T(1,128)}), f32[1,512,128]{2,0,1:T(1,128)S(1)}, u32[]{:S(2)}, u32[]{:S(2)}) async-start(f32[1,512,128]{2,0,1:T(1,128)} %bitcast.2), calls=%async_computation | async-start | bytes 524288 | tf_op jit(solution)/shard_map/all_to_all | solution.py:23
  30.1 21.6 %all-to-all-start.3 = ((f32[1,512,256]{2,0,1:T(1,128)}), f32[1,512,256]{2,0,1:T(1,128)S(1)}, u32[]{:S(2)}, u32[]{:S(2)}) async-start(f32[1,512,256]{2,0,1:T(1,128)} %broadcast_in_dim.7), calls=%async_computation.3 | async-start | bytes 1048576 | tf_op jit(solution)/shard_map/all_to_all | solution.py:23
  51.7 21.9 %all-to-all-start.9 = ((f32[1,512,256]{2,0,1:T(1,128)}), f32[1,512,256]{2,0,1:T(1,128)S(1)}, u32[]{:S(2)}, u32[]{:S(2)}) async-start(f32[1,512,256]{2,0,1:T(1,128)} %broadcast_in_dim.8), calls=%async_computation.9 | async-start | bytes 1048576 | tf_op jit(solution)/shard_map/all_to_all | solution.py:23
  73.6 21.9 %all-to-all-start.2 = ((f32[64,16,128]{2,1,0:T(8,128)}), f32[64,16,128]{2,1,0:T(8,128)S(1)}, u32[]{:S(2)}, u32[]{:S(2)}) async-start(f32[64,16,128]{2,1,0:T(8,128)} %copy.110), calls=%async_computation.2 | async-start | bytes 1048576 | tf_op jit(solution)/shard_map/all_to_all | solution.py:35
  95.5 8.3 %copy-start.9 = (f32[64,16,128]{2,1,0:T(8,128)}, f32[64,16,128]{2,1,0:T(8,128)S(1)}, u32[]{:S(2)}) copy-start(f32[64,16,128]{2,1,0:T(8,128)S(1)} %all-to-all-done.2) | copy-start | bytes 1572868
  95.5 22.6 %all-to-all-start.1 = ((f32[64,16,128]{2,1,0:T(8,128)}), f32[64,16,128]{2,1,0:T(8,128)}, u32[]{:S(2)}, u32[]{:S(2)}) async-start(f32[64,16,128]{2,1,0:T(8,128)} %copy.107), calls=%async_computation.1 | async-start | bytes 1048576 | tf_op jit(solution)/shard_map/all_to_all | solution.py:34
  118.1 34.1 %all-to-all-start.10 = ((f32[64,16,256]{2,1,0:T(8,128)}), f32[64,16,256]{2,1,0:T(8,128)}, u32[]{:S(2)}, u32[]{:S(2)}) async-start(f32[64,16,256]{2,1,0:T(8,128)} %copy.134), calls=%async_computation.10 | async-start | bytes 2097152 | tf_op jit(solution)/shard_map/all_to_all | solution.py:34
  152.1 33.1 %all-to-all-start.11 = ((f32[64,16,256]{2,1,0:T(8,128)}), f32[64,16,256]{2,1,0:T(8,128)S(1)}, u32[]{:S(2)}, u32[]{:S(2)}) async-start(f32[64,16,256]{2,1,0:T(8,128)} %copy.137), calls=%async_computation.11 | async-start | bytes 2097152 | tf_op jit(solution)/shard_map/all_to_all | solution.py:35
  185.3 33.1 %all-to-all-start.4 = ((f32[64,16,256]{2,1,0:T(8,128)}), f32[64,16,256]{2,1,0:T(8,128)S(1)}, u32[]{:S(2)}, u32[]{:S(2)}) async-start(f32[64,16,256]{2,1,0:T(8,128)} %copy.115), calls=%async_computation.4 | async-start | bytes 2097152 | tf_op jit(solution)/shard_map/all_to_all | solution.py:34
  218.4 65.7 %all-to-all-start.5 = ((f32[64,16,256]{2,1,0:T(8,128)}), f32[64,16,256]{2,1,0:T(8,128)S(1)}, u32[]{:S(2)}, u32[]{:S(2)}) async-start(f32[64,16,256]{2,1,0:T(8,128)} %copy.118), calls=%async_computation.5 | async-start | bytes 2097152 | tf_op jit(solution)/shard_map/all_to_all | solution.py:35
  291.7 7.8 %copy-start.17 = (f32[2,32,16,256]{3,2,1,0:T(8,128)S(1)}, f32[2,32,16,256]{3,2,1,0:T(8,128)}, u32[]{:S(2)}) copy-start(f32[2,32,16,256]{3,2,1,0:T(8,128)} %copy-done.16) | copy-start | bytes 3145732
  291.7 7.8 %copy-start.26 = (f32[2,256,512]{2,1,0:T(8,128)S(1)}, f32[2,256,512]{2,1,0:T(8,128)}, u32[]{:S(2)}) copy-start(f32[2,256,512]{2,1,0:T(8,128)} %fusion.36) | copy-start | bytes 3145732
  299.6 7.6 %copy-start.15 = (f32[2,512,256]{1,2,0:T(8,128)S(1)}, f32[2,512,256]{1,2,0:T(8,128)}, u32[]{:S(2)}) copy-start(f32[2,512,256]{1,2,0:T(8,128)} %fusion.1) | copy-start | bytes 3145732
  299.6 7.6 %copy-start.23 = (f32[2,512,128]{1,2,0:T(8,128)S(1)}, f32[2,512,128]{1,2,0:T(8,128)}, u32[]{:S(2)}) copy-start(f32[2,512,128]{1,2,0:T(8,128)} %fusion.4) | copy-start | bytes 1572868
  341.6 10.6 %copy-start.12 = (f32[2,512,256]{1,2,0:T(8,128)S(1)}, f32[2,512,256]{1,2,0:T(8,128)}, u32[]{:S(2)}) copy-start(f32[2,512,256]{1,2,0:T(8,128)} %get-tuple-element.18) | copy-start | bytes 3145732
  342.6 29.4 %all-to-all-start.15 = ((f32[2,512,128]{2,0,1:T(2,128)}), f32[2,512,128]{2,0,1:T(2,128)S(1)}, u32[]{:S(2)}, u32[]{:S(2)}) async-start(f32[2,512,128]{2,0,1:T(2,128)} %copy.149), calls=%async_computation.15 | async-start | bytes 1048576 | tf_op jit(solution)/shard_map/all_to_all | solution.py:64
  365.3 15.3 %copy-start.4 = (f32[2,512,256]{1,2,0:T(8,128)S(1)}, f32[2,512,256]{1,2,0:T(8,128)}, u32[]{:S(2)}) copy-start(f32[2,512,256]{1,2,0:T(8,128)} %get-tuple-element.20) | copy-start | bytes 3145732
  372.0 29.3 %all-to-all-start.16 = ((f32[2,512,128]{2,0,1:T(2,128)}), f32[2,512,128]{2,0,1:T(2,128)S(1)}, u32[]{:S(2)}, u32[]{:S(2)}) async-start(f32[2,512,128]{2,0,1:T(2,128)} %copy.152), calls=%async_computation.16 | async-start | bytes 1048576 | tf_op jit(solution)/shard_map/all_to_all | solution.py:65
  403.1 24.7 %all-to-all-start.17 = ((f32[32,16,128]{2,1,0:T(8,128)}), f32[32,16,128]{2,1,0:T(8,128)S(1)}, u32[]{:S(2)}, u32[]{:S(2)}) async-start(f32[32,16,128]{2,1,0:T(8,128)} %copy.155), calls=%async_computation.17 | async-start | bytes 524288 | tf_op jit(solution)/shard_map/all_to_all | solution.py:74
  427.8 9.6 %copy-start.18 = (f32[32,16,128]{2,1,0:T(8,128)}, f32[32,16,128]{2,1,0:T(8,128)S(1)}, u32[]{:S(2)}) copy-start(f32[32,16,128]{2,1,0:T(8,128)S(1)} %all-to-all-done.17) | copy-start | bytes 786436
  427.8 36.3 %all-to-all-start.12 = ((f32[2,512,256]{2,0,1:T(2,128)}), f32[2,512,256]{2,0,1:T(2,128)S(1)}, u32[]{:S(2)}, u32[]{:S(2)}) async-start(f32[2,512,256]{2,0,1:T(2,128)} %copy.142), calls=%async_computation.12 | async-start | bytes 2097152 | tf_op jit(solution)/shard_map/all_to_all | solution.py:64
  464.1 32.5 %all-to-all-start.6 = ((f32[2,512,256]{2,0,1:T(2,128)}), f32[2,512,256]{2,0,1:T(2,128)S(1)}, u32[]{:S(2)}, u32[]{:S(2)}) async-start(f32[2,512,256]{2,0,1:T(2,128)} %copy.125), calls=%async_computation.6 | async-start | bytes 2097152 | tf_op jit(solution)/shard_map/all_to_all | solution.py:64
  496.6 33.1 %all-to-all-start.7 = ((f32[2,512,256]{2,0,1:T(2,128)}), f32[2,512,256]{2,0,1:T(2,128)S(1)}, u32[]{:S(2)}, u32[]{:S(2)}) async-start(f32[2,512,256]{2,0,1:T(2,128)} %copy.128), calls=%async_computation.7 | async-start | bytes 2097152 | tf_op jit(solution)/shard_map/all_to_all | solution.py:65
  530.8 33.1 %all-to-all-start.13 = ((f32[2,512,256]{2,0,1:T(2,128)}), f32[2,512,256]{2,0,1:T(2,128)S(1)}, u32[]{:S(2)}, u32[]{:S(2)}) async-start(f32[2,512,256]{2,0,1:T(2,128)} %copy.145), calls=%async_computation.13 | async-start | bytes 2097152 | tf_op jit(solution)/shard_map/all_to_all | solution.py:65
  535.8 73.6 %all-gather.2.cloned.1.call-start = ((), (), s32[]{:S(2)}) async-start(), calls=%async_computation.18 | async-start | bytes 2359296 | tf_op jit(solution)/shard_map/all_gather | solution.py:121
  563.9 22.6 %all-to-all-start.8 = ((f32[32,16,256]{2,1,0:T(8,128)}), f32[32,16,256]{2,1,0:T(8,128)}, u32[]{:S(2)}, u32[]{:S(2)}) async-start(f32[32,16,256]{2,1,0:T(8,128)} %copy.131), calls=%async_computation.8 | async-start | bytes 1048576 | tf_op jit(solution)/shard_map/all_to_all | solution.py:74
  573.5 18.0 %copy-start.6 = (f32[512,256]{1,0:T(8,128)S(1)}, f32[512,256]{1,0:T(8,128)}, u32[]{:S(2)}) copy-start(f32[512,256]{1,0:T(8,128)} %param.9) | copy-start | bytes 1572868
  574.2 34.1 %copy-start.7 = (f32[512,256]{1,0:T(8,128)S(1)}, f32[512,256]{1,0:T(8,128)}, u32[]{:S(2)}) copy-start(f32[512,256]{1,0:T(8,128)} %param.6) | copy-start | bytes 1572868
  574.3 34.1 %copy-start.8 = (f32[512,256]{1,0:T(8,128)S(1)}, f32[512,256]{1,0:T(8,128)}, u32[]{:S(2)}) copy-start(f32[512,256]{1,0:T(8,128)} %param.7) | copy-start | bytes 1572868
  586.5 21.9 %all-to-all-start.14 = ((f32[32,16,256]{2,1,0:T(8,128)}), f32[32,16,256]{2,1,0:T(8,128)S(1)}, u32[]{:S(2)}, u32[]{:S(2)}) async-start(f32[32,16,256]{2,1,0:T(8,128)} %copy.148), calls=%async_computation.14 | async-start | bytes 1048576 | tf_op jit(solution)/shard_map/all_to_all | solution.py:74
  (17 other events, 86.3 us)
Sparse Core Ops, SparseCore 0:
  539.8 62.7 all-gather.1
